TPU v7x, 32 devices: a whole 2x2x4 slice. The times are simulated.
32 devices in a mesh: parts: 2 (over x), tm: 16 (over z, y, core).
Axes of the slice: x: 2, y: 2, z: 4, core: 2. Of those that a mesh axis runs over, the one named last changes fastest.
Arguments:
- currents: bfloat16 [49152, 1024], P('tm', 'parts'), parts along dimension 1, may hold values from -5 to 5
- seed_on_tension: bfloat16 [49152, 1024], P('tm', 'parts'), parts along dimension 1, may hold values from -6 to 6
- mode_diffusivity_factor: float32 [32, 98304], P(None, ('parts', 'tm')), parts along dimension 1, may hold values from 0.25 to 34410
- decay_rates: float32 [32], replicated, may hold values from 6.1035156e-06 to 0.34
- fit_weights: float32 [32], replicated, may hold values from 0.06 to 0.3
- counts: int32 [1024], P('parts'), parts along dimension 0, may hold values from 1 to 16
Outputs:
- tension_at_end: bfloat16 [49152, 1024], P('tm', 'parts'), parts along dimension 1
- gradient_wrt_draw: bfloat16 [49152, 1024], P('tm', 'parts'), parts along dimension 1
- softened_peak_tension: float32 [1024], P('parts'), parts along dimension 0
There are 2 independent parts, one for each index of `parts`. A program takes and returns all parts, laid end to end along the dimension named above; an argument that names none is the same for every part. Nothing has to cross between parts.
All inputs are finite; a program needn't handle non-finite values.
Results may differ from a plain program's by a relative error of at most 0.0053.
Values sent between devices are 32-bit elements; how exact they have to be, the bound alone decides.
No kernel may reach another device: no remote copies, remote signals or barrier semaphores. Data moves between devices by JAX's collectives and lax.ppermute only.
A program may use at most 192 MiB of HBM per device.

v0:
```python
import jax
import jax.numpy as jnp
from jax import lax
from jax.sharding import PartitionSpec as P

KERNEL_SPAN = 768
SHARPNESS = 4.0
FAR_AWAY = 1e30


def entering(part, axis, combine, identity, reverse):
    count = lax.axis_size(axis)
    place = lax.axis_index(axis)
    ahead = count - 1 - place if reverse else place
    gathered = jax.tree.map(lambda a: lax.all_gather(a, axis), part)
    state = jax.tree.map(lambda a, e: jnp.zeros_like(a) + jnp.asarray(e, a.dtype), part, identity)

    def one(hop, state):
        source = count - 1 - hop if reverse else hop
        return combine(
            state, jax.tree.map(lambda a: lax.dynamic_index_in_dim(a, source, 0, False), gathered)
        )

    return lax.fori_loop(0, ahead, one, state)


def combine_states(earlier, latter):
    return (earlier[0] * latter[0], latter[0][:, None] * earlier[1] + latter[1])


def body(currents, seed_on_tension, mode_diffusivity_factor, decay_rates, fit_weights, counts):
    samples, conductor_total = currents.shape
    kernel_spans = samples // KERNEL_SPAN
    mode_count = decay_rates.shape[0]
    mode_gains = fit_weights * jnp.sqrt(decay_rates)
    length_scale = counts.astype(jnp.float32) / 4.0
    prefix = jnp.cumsum(
        mode_diffusivity_factor.reshape(mode_count, kernel_spans, KERNEL_SPAN), axis=2
    ).transpose(1, 0, 2)
    closing_instant = prefix[:, :, -1]
    prefix_rows = prefix.transpose(0, 2, 1)
    row_ids = lax.broadcasted_iota(jnp.int32, (KERNEL_SPAN, KERNEL_SPAN), 0)
    col_ids = lax.broadcasted_iota(jnp.int32, (KERNEL_SPAN, KERNEL_SPAN), 1)
    lower_part = (row_ids >= col_ids)[None]
    kernel_list = []
    for position in range(kernel_spans):
        block_kernel = jnp.zeros((KERNEL_SPAN, KERNEL_SPAN), jnp.float32)
        for first_mode in range(0, mode_count, 8):
            rate_part = decay_rates[first_mode : first_mode + 8]
            gain_part = mode_gains[first_mode : first_mode + 8]
            part_prefix = prefix[position, first_mode : first_mode + 8]
            spread = part_prefix[:, :, None] - part_prefix[:, None, :]
            spread = jnp.where(lower_part, spread, FAR_AWAY)
            block_kernel = block_kernel + jnp.sum(
                gain_part[:, None, None] * jnp.exp(-rate_part[:, None, None] * spread), axis=0
            )
        kernel_list.append(block_kernel.astype(jnp.bfloat16))
    kernel = jnp.stack(kernel_list)
    back_table = jnp.exp(-decay_rates[None, None, :] * (closing_instant[:, None, :] - prefix_rows))
    start_table = mode_gains * jnp.exp(-decay_rates * prefix_rows)
    decays = jnp.exp(-decay_rates[None, :] * closing_instant)
    cur_blocks = currents.reshape(kernel_spans, KERNEL_SPAN, conductor_total)
    cot_blocks = seed_on_tension.reshape(kernel_spans, KERNEL_SPAN, conductor_total)
    local_fwd = jnp.einsum("bts,bsw->btw", kernel, cur_blocks, preferred_element_type=jnp.float32)
    fresh_fwd = jnp.einsum(
        "bsm,bsw->bmw",
        back_table.astype(jnp.bfloat16),
        cur_blocks,
        preferred_element_type=jnp.float32,
    )
    local_adj = jnp.einsum("bts,btw->bsw", kernel, cot_blocks, preferred_element_type=jnp.float32)
    fresh_adj = jnp.einsum(
        "btm,btw->bmw",
        start_table.astype(jnp.bfloat16),
        cot_blocks,
        preferred_element_type=jnp.float32,
    )
    dev_decay = jnp.ones((mode_count,), jnp.float32)
    resident_mode_values = jnp.zeros((mode_count, conductor_total), jnp.float32)
    for position in range(kernel_spans):
        dev_decay = dev_decay * decays[position]
        resident_mode_values = (
            decays[position][:, None] * resident_mode_values + fresh_fwd[position]
        )
    shard_adjoint_rows = jnp.zeros((mode_count, conductor_total), jnp.float32)
    for position in reversed(range(kernel_spans)):
        shard_adjoint_rows = decays[position][:, None] * shard_adjoint_rows + fresh_adj[position]
    no_decay = jnp.ones((mode_count,), jnp.float32)
    no_state = jnp.zeros((mode_count, conductor_total), jnp.float32)
    forward_pair = entering(
        (dev_decay, resident_mode_values), "tm", combine_states, (no_decay, no_state), False
    )
    adjoint_pair = entering(
        (dev_decay, shard_adjoint_rows), "tm", combine_states, (no_decay, no_state), True
    )
    state_in = forward_pair[1]
    adjoint_in = adjoint_pair[1]
    mode_state = state_in
    full_blocks = []
    for position in range(kernel_spans):
        carried_in = jnp.dot(
            start_table[position],
            mode_state,
            precision=lax.Precision.HIGHEST,
            preferred_element_type=jnp.float32,
        )
        full_blocks.append(length_scale[None, :] * (local_fwd[position] + carried_in))
        if position + 1 < kernel_spans:
            mode_state = decays[position][:, None] * mode_state + fresh_fwd[position]
    stress_full = jnp.stack(full_blocks)
    scores = SHARPNESS * stress_full
    local_high = jnp.max(scores, axis=(0, 1))
    highest = lax.pmax(local_high, "tm")
    amount = lax.psum(jnp.sum(jnp.exp(scores - highest), axis=(0, 1)), "tm")
    softened_peak_tension = (highest + jnp.log(amount)) / SHARPNESS
    adjoint_state = adjoint_in
    reversed_blocks = []
    for position in reversed(range(kernel_spans)):
        carried_in = jnp.dot(
            back_table[position],
            adjoint_state,
            precision=lax.Precision.HIGHEST,
            preferred_element_type=jnp.float32,
        )
        reversed_blocks.append(
            (length_scale[None, :] * (local_adj[position] + carried_in)).astype(jnp.bfloat16)
        )
        if position > 0:
            adjoint_state = decays[position][:, None] * adjoint_state + fresh_adj[position]
    gradient_wrt_draw = jnp.stack(reversed_blocks[::-1]).reshape(samples, conductor_total)
    tension_at_end = stress_full.astype(jnp.bfloat16).reshape(samples, conductor_total)
    return (tension_at_end, gradient_wrt_draw, softened_peak_tension)


def solution(mesh):
    placed = (P("tm", "parts"), P("tm", "parts"), P(None, ("parts", "tm")), P(), P(), P("parts"))
    return jax.shard_map(
        body,
        mesh=mesh,
        in_specs=placed,
        out_specs=(P("tm", "parts"), P("tm", "parts"), P("parts")),
        check_vma=False,
    )
```

profile of v0, /device:TPU:0, one launch (start us, length us, event | category | flops | bytes accessed | tf_op | source)
XLA Modules:
  0.0 303.3 jit_solution(5276616047635515305)
XLA Ops:
  7.2 2.1 reshape.270
  9.4 2.0 copy.54
  11.4 12.3 %reduce-window.6 = f32[32,4,6,128]{3,0,1,2:T(8,128)S(1)} reduce-window(f32[32,4,6,128]{3,0,1,2:T(8,128)} %copy.54, f32[]{:T(128)} %constant.65.clone.1), window={size=1x1x1x128 pad=0_0x0_0x0_0x127_0}, to_apply=%region_0.0 | reduce-window | flops 12484608 | bytes 786436 | tf_op jit(solution)/shard_map/reduce-window
  24.4 0.7 fusion.53
  26.0 2.8 fusion.41
  29.4 0.7 copy-done.14
  30.1 0.8 slice_add_fusion
  31.0 0.7 all-gather.6.cloned.1.call-update
  31.7 1.6 slice_bitcast_fusion.27
  33.4 0.6 slice_negate_fusion.3
  34.3 22.8 %multiply_reduce_fusion.15 = (f32[768,768]{1,0:T(8,128)}, f32[768,768]{1,0:T(8,128)}, f32[768,768]{1,0:T(8,128)}, f32[768,768]{1,0:T(8,128)}) fusion(f32[8,768]{1,0:T(8,128)S(1)} %get-tuple-element.194, f32[8]{0:T(128)S(1)} %get-tuple-element.210, f32[8]{0:T(128)S(1)} %get-tuple-element.206, pred[768,768]{1,0:T(8,128)(4,1)S(1)} %iota_compare_fusion, ...), kind=kLoop, calls=%fused_computation.19 | loop fusion | flops 92012544 | bytes 10125376 | tf_op jit(solution)/shard_map/reduce_sum | solution.py:54
  57.0 72.1 %multiply_reduce_fusion.14 = (f32[768,768]{1,0:T(8,128)}, f32[768,768]{1,0:T(8,128)}, f32[768,768]{1,0:T(8,128)}, f32[768,768]{1,0:T(8,128)}, f32[768,768]{1,0:T...) fusion(f32[8,768]{1,0:T(8,128)} %get-tuple-element.193, ...), kind=kLoop, calls=%fused_computation.18 | loop fusion | flops 276037632 | bytes 29196480 | tf_op jit(solution)/shard_map/reduce_sum | solution.py:54
  129.1 9.0 %fusion.28 = (bf16[1,768,768]{2,1,0:T(8,128)(2,1)}, bf16[1,768,768]{2,1,0:T(8,128)(2,1)}) fusion(f32[768,768]{1,0:T(8,128)} %get-tuple-element.156, f32[768,768]{1,0:T(8,128)} %get-tuple-element.152, f32[768,768]{1,0:T(8,128)} %get-tuple-element.137, f32[768,768]{1,0:T(8,128)} %get-tuple-element.133, f32[768,768]{1,0:T(8,128)} %get-tuple-element.155, ...), kind=kLoop, calls=%fused_computation.66 | loop fusion | flops 4718592 | bytes 21233664 | tf_op jit(solution)/shard_map/convert_element_type | solution.py:57
  138.1 7.1 %fusion.30 = (bf16[1,768,768]{2,1,0:T(8,128)(2,1)}, bf16[1,768,768]{2,1,0:T(8,128)(2,1)}) fusion(f32[768,768]{1,0:T(8,128)} %get-tuple-element.154, f32[768,768]{1,0:T(8,128)} %get-tuple-element.150, f32[768,768]{1,0:T(8,128)S(1)} %copy-done.11, f32[768,768]{1,0:T(8,128)S(1)} %copy-done.13, f32[768,768]{1,0:T(8,128)} %get-tuple-element.153, ...), kind=kLoop, calls=%fused_computation.68 | loop fusion | flops 4718592 | bytes 21233664 | tf_op jit(solution)/shard_map/convert_element_type | solution.py:57
  145.3 7.8 %fusion.34 = f32[4,768,512]{2,1,0:T(8,128)} fusion(bf16[4,768,512]{2,1,0:T(8,128)(2,1)S(1)} %bitcast.251, bf16[1,768,768]{2,1,0:T(8,128)(2,1)} %get-tuple-element.217, bf16[1,768,768]{2,1,0:T(8,128)(2,1)} %get-tuple-element.216, bf16[1,768,768]{2,1,0:T(8,128)(2,1)} %get-tuple-element.215, bf16[1,768,768]{2,1,0:T(8,128)(2,1)} %get-tuple-element.214), kind=kOutput, calls=%fused_computation.72 | convolution fusion | flops 2422996992 | bytes 14155776 | tf_op jit(solution)/shard_map/bts,bsw->btw/dot_general | solution.py:64
  153.1 4.8 %fusion.33 = f32[4,768,512]{2,1,0:T(8,128)} fusion(bf16[4,768,512]{2,1,0:T(8,128)(2,1)S(1)} %bitcast.255, bf16[1,768,768]{2,1,0:T(8,128)(2,1)S(1)} %copy-done.19, bf16[1,768,768]{2,1,0:T(8,128)(2,1)S(1)} %copy-done.18, bf16[1,768,768]{2,1,0:T(8,128)(2,1)S(1)} %copy-done.17, bf16[1,768,768]{2,1,0:T(8,128)(2,1)S(1)} %copy-done.16), kind=kOutput, calls=%fused_computation.71 | convolution fusion | flops 2422996992 | bytes 14155776 | tf_op jit(solution)/shard_map/bts,btw->bsw/dot_general | solution.py:71
  157.9 23.1 %all-gather = f32[16,1,32]{2,1,0:T(1,128)S(1)} all-gather(f32[1,1,32]{2,1,0:T(1,128)S(1)} %copy-done.28), channel_id=1, replica_groups=mesh['parts'=2,'tm'=16] {'tm'}, dimensions={0}, use_global_device_ids=true | all-gather | bytes 2176 | tf_op jit(solution)/shard_map/all_gather | solution.py:15
  181.1 4.3 %fusion.23 = f32[1,768,512]{2,1,0:T(8,128)} fusion(f32[4,768,512]{2,1,0:T(8,128)} %fusion.34, f32[32,512]{1,0:T(8,128)S(1)} %get-tuple-element.131, f32[512]{0:T(512)S(1)} %convert_multiply_fusion, f32[4,768,32]{1,2,0:T(8,128)} %copy-done.8), kind=kOutput, calls=%fused_computation.61 | convolution fusion | flops 151781376 | bytes 3311616 | tf_op jit(solution)/shard_map/dot_general | solution.py:101
  185.4 1.0 bitcast_add_fusion.8
  186.3 4.1 %fusion.17 = f32[1,768,512]{2,1,0:T(8,128)} fusion(f32[4,768,512]{2,1,0:T(8,128)} %fusion.34, f32[32,512]{1,0:T(8,128)S(1)} %bitcast_add_fusion.8, f32[512]{0:T(512)S(1)} %convert_multiply_fusion, f32[4,768,32]{1,2,0:T(8,128)} %copy-done.8), kind=kOutput, calls=%fused_computation.53 | convolution fusion | flops 151781376 | bytes 3311616 | tf_op jit(solution)/shard_map/dot_general | solution.py:101
  190.4 3.5 %fusion.20 = f32[1,768,512]{2,1,0:T(8,128)} fusion(f32[4,768,512]{2,1,0:T(8,128)S(1)} %copy-done.5, f32[512]{0:T(512)S(1)} %convert_multiply_fusion, f32[4,768,32]{1,2,0:T(8,128)S(1)} %copy-done.9, f32[32,512]{1,0:T(8,128)S(1)} %get-tuple-element.131, f32[4,32,512]{2,1,0:T(8,128)} %copy-done.14, f32[32]{0:T(128)S(1)} %copy-done.27), kind=kOutput, calls=%fused_computation.57 | convolution fusion | flops 151814144 | bytes 3377664 | tf_op jit(solution)/shard_map/dot_general | solution.py:101
  193.9 3.5 %fusion.14 = f32[1,768,512]{2,1,0:T(8,128)} fusion(f32[4,768,512]{2,1,0:T(8,128)S(1)} %copy-done.5, f32[512]{0:T(512)S(1)} %convert_multiply_fusion, f32[4,768,32]{1,2,0:T(8,128)S(1)} %copy-done.9, f32[32,512]{1,0:T(8,128)S(1)} %bitcast_add_fusion.8, f32[4,32,512]{2,1,0:T(8,128)} %copy-done.14, f32[32]{0:T(128)S(1)} %copy-done.25), kind=kOutput, calls=%fused_computation.49 | convolution fusion | flops 151814144 | bytes 3377664 | tf_op jit(solution)/shard_map/dot_general | solution.py:101
  197.3 14.0 %while.27 = (s32[]{:T(128)}, f32[32,512]{1,0:T(8,128)S(1)}, s32[]{:T(128)}, f32[16,32]{1,0:T(8,128)S(1)}, f32[16,32,512]{2,1,0:T(8,128)}, /*index=5*/s32[]{:T(128)}, s32[]{:T(128)}, s32[]{:T(128)}, s32[]{:T(128)}) while((s32[]{:T(128)}, f32[32,512]{1,0:T(8,128)S(1)}, s32[]{:T(128)}, f32[16,32]{1,0:T(8,128)S(1)}, f32[16,32,512]{2,1,0:T(8,128)}, ...), condition=%wide.region_21.22_spmd, body=%wide.region_20.21_spmd.sunk | while | flops 32774 | bytes 197139 | solution.py:24
  197.4 0.9 bitcast_add_fusion.15
  198.3 0.9 bitcast_add_fusion.15
  199.2 0.9 bitcast_add_fusion.15
  200.2 0.9 bitcast_add_fusion.15
  201.1 0.9 bitcast_add_fusion.15
  202.0 0.9 bitcast_add_fusion.15
  203.0 0.9 bitcast_add_fusion.15
  203.9 0.9 bitcast_add_fusion.15
  204.8 0.9 bitcast_add_fusion.15
  205.8 0.9 bitcast_add_fusion.15
  206.7 0.9 bitcast_add_fusion.15
  207.6 0.9 bitcast_add_fusion.15
  208.6 0.9 bitcast_add_fusion.15
  209.5 0.9 bitcast_add_fusion.15
  210.4 0.9 bitcast_add_fusion.15
  211.5 4.1 %fusion.24 = bf16[1,768,512]{2,1,0:T(8,128)(2,1)} fusion(f32[4,768,512]{2,1,0:T(8,128)} %fusion.33, f32[512]{0:T(512)S(1)} %convert_multiply_fusion, f32[4,768,32]{1,2,0:T(8,128)} %copy-done.6, f32[32,512]{1,0:T(8,128)S(1)} %bitcast_add_fusion.4, f32[4,32,512]{2,1,0:T(8,128)S(1)} %fusion.41, f32[32]{0:T(128)S(1)} %copy-done.23), kind=kOutput, calls=%fused_computation.62 | convolution fusion | flops 152207360 | bytes 2591232 | tf_op jit(solution)/shard_map/dot_general | solution.py:119
  215.5 3.9 %fusion.25 = bf16[1,768,512]{2,1,0:T(8,128)(2,1)} fusion(f32[32,512]{1,0:T(8,128)S(1)} %bitcast_add_fusion.4, f32[4,768,512]{2,1,0:T(8,128)} %fusion.33, f32[512]{0:T(512)S(1)} %convert_multiply_fusion, f32[4,768,32]{1,2,0:T(8,128)} %copy-done.6), kind=kOutput, calls=%fused_computation.63 | convolution fusion | flops 152174592 | bytes 2525184 | tf_op jit(solution)/shard_map/dot_general | solution.py:119
  219.4 3.8 %fusion.26 = bf16[1,768,512]{2,1,0:T(8,128)(2,1)} fusion(f32[4,768,512]{2,1,0:T(8,128)} %fusion.33, f32[512]{0:T(512)S(1)} %convert_multiply_fusion, f32[4,768,32]{1,2,0:T(8,128)S(1)} %copy-done.7, f32[32,512]{1,0:T(8,128)S(1)} %get-tuple-element.132, f32[4,32,512]{2,1,0:T(8,128)S(1)} %fusion.41, f32[32]{0:T(128)S(1)} %get-tuple-element.198), kind=kOutput, calls=%fused_computation.64 | convolution fusion | flops 152207360 | bytes 2591232 | tf_op jit(solution)/shard_map/dot_general | solution.py:119
  223.2 3.8 %fusion.27 = bf16[1,768,512]{2,1,0:T(8,128)(2,1)} fusion(f32[32,512]{1,0:T(8,128)S(1)} %get-tuple-element.132, f32[4,768,512]{2,1,0:T(8,128)} %fusion.33, f32[512]{0:T(512)S(1)} %convert_multiply_fusion, f32[4,768,32]{1,2,0:T(8,128)S(1)} %copy-done.7), kind=kOutput, calls=%fused_computation.65 | convolution fusion | flops 152174592 | bytes 2525184 | tf_op jit(solution)/shard_map/dot_general | solution.py:119
  227.0 0.9 multiply_reduce_fusion.16
  227.9 2.1 fusion.32
  229.9 29.8 %pmax.7 = f32[512]{0:T(512)S(1)} all-reduce(f32[512]{0:T(512)S(1)} %multiply_reduce_fusion.16), channel_id=1, replica_groups=mesh['parts'=2,'tm'=16] {'tm'}, use_global_device_ids=true, to_apply=%region_23.24 | all-reduce | flops 512 | bytes 4096 | tf_op jit(solution)/shard_map/pmax | solution.py:113
  259.7 3.4 %exponential_reduce_fusion = f32[512]{0:T(512)S(1)} fusion(f32[512]{0:T(512)S(1)} %pmax.7, f32[1,768,512]{2,1,0:T(8,128)} %fusion.14, f32[1,768,512]{2,1,0:T(8,128)} %fusion.17, f32[1,768,512]{2,1,0:T(8,128)} %fusion.20, f32[1,768,512]{2,1,0:T(8,128)} %fusion.23), kind=kLoop, calls=%fused_computation.21 | loop fusion | flops 9436672 | bytes 6295552 | tf_op jit(solution)/shard_map/reduce_sum | solution.py:114
  263.1 29.5 %psum.7 = f32[512]{0:T(512)S(1)} all-reduce(f32[512]{0:T(512)S(1)} %exponential_reduce_fusion), channel_id=1, replica_groups=mesh['parts'=2,'tm'=16] {'tm'}, use_global_device_ids=true, to_apply=%region_25.26 | all-reduce | flops 512 | bytes 4096 | tf_op jit(solution)/shard_map/psum | solution.py:114
  293.2 3.2 %pad_maximum_fusion.2 = bf16[4,768,512]{2,1,0:T(8,128)(2,1)} fusion(bf16[1,768,512]{2,1,0:T(8,128)(2,1)} %fusion.27, bf16[1,768,512]{2,1,0:T(8,128)(2,1)} %fusion.26, bf16[1,768,512]{2,1,0:T(8,128)(2,1)} %fusion.25, bf16[1,768,512]{2,1,0:T(8,128)(2,1)} %fusion.24), kind=kLoop, calls=%fused_computation.24 | loop fusion | flops 4718592 | bytes 6291456 | tf_op jit(solution)/shard_map/stack | solution.py:130
  (99 shorter events, 3.4 us)
Async XLA Ops:
  7.2 21.6 %copy-start = (bf16[3072,512]{1,0:T(8,128)(2,1)S(1)}, bf16[3072,512]{1,0:T(8,128)(2,1)}, u32[]{:S(2)}) copy-start(bf16[3072,512]{1,0:T(8,128)(2,1)} %param.10) | copy-start | bytes 9437188
  7.2 173.9 %all-gather.4.cloned.1.call-start = ((), (), s32[]{:S(2)}) async-start(), calls=%async_computation | async-start | bytes 1114112 | tf_op jit(solution)/shard_map/all_gather | solution.py:15
  24.2 1.7 copy-start.15
  25.7 5.2 %copy-start.22 = (f32[32]{0:T(128)}, f32[32]{0:T(128)S(1)}, u32[]{:S(2)}) copy-start(f32[32]{0:T(128)S(1)} %get-tuple-element.201) | copy-start | bytes 388
  25.7 5.2 %copy-start.24 = (f32[32]{0:T(128)}, f32[32]{0:T(128)S(1)}, u32[]{:S(2)}) copy-start(f32[32]{0:T(128)S(1)} %get-tuple-element.200) | copy-start | bytes 388
  25.7 5.2 %copy-start.26 = (f32[32]{0:T(128)}, f32[32]{0:T(128)S(1)}, u32[]{:S(2)}) copy-start(f32[32]{0:T(128)S(1)} %get-tuple-element.197) | copy-start | bytes 388
  25.9 2.9 copy-start.6
  25.9 3.5 %copy-start.8 = (f32[4,768,32]{1,2,0:T(8,128)}, f32[4,768,32]{1,2,0:T(8,128)S(1)}, u32[]{:S(2)}) copy-start(f32[4,768,32]{1,2,0:T(8,128)S(1)} %get-tuple-element.178) | copy-start | bytes 1179652
  25.9 7.5 %copy-start.21 = (f32[32]{0:T(128)S(1)}, f32[32]{0:T(128)}, u32[]{:S(2)}) copy-start(f32[32]{0:T(128)} %param.13) | copy-start | bytes 388
  29.4 0.7 copy-start.14
  30.9 166.4 %all-gather.6.cloned.1.call-start = ((), (), s32[]{:S(2)}) async-start(), calls=%async_computation.1 | async-start | bytes 1114112 | tf_op jit(solution)/shard_map/all_gather | solution.py:15
  34.2 22.8 %copy-start.20 = (pred[768,768]{1,0:T(8,128)(4,1)}, pred[768,768]{1,0:T(8,128)(4,1)S(1)}, u32[]{:S(2)}) copy-start(pred[768,768]{1,0:T(8,128)(4,1)S(1)} %iota_compare_fusion) | copy-start | bytes 1769476
  34.2 22.8 %copy-start.30 = (f32[8]{0:T(128)S(1)}, f32[8]{0:T(128)}, u32[]{:S(2)}) copy-start(f32[8]{0:T(128)} %get-tuple-element.212) | copy-start | bytes 100
  129.1 9.0 %copy-start.11 = (f32[768,768]{1,0:T(8,128)S(1)}, f32[768,768]{1,0:T(8,128)}, u32[]{:S(2)}) copy-start(f32[768,768]{1,0:T(8,128)} %get-tuple-element.139) | copy-start | bytes 7077892
  129.1 9.0 %copy-start.12 = (f32[768,768]{1,0:T(8,128)S(1)}, f32[768,768]{1,0:T(8,128)}, u32[]{:S(2)}) copy-start(f32[768,768]{1,0:T(8,128)} %get-tuple-element.140) | copy-start | bytes 7077892
  129.1 9.0 %copy-start.13 = (f32[768,768]{1,0:T(8,128)S(1)}, f32[768,768]{1,0:T(8,128)}, u32[]{:S(2)}) copy-start(f32[768,768]{1,0:T(8,128)} %get-tuple-element.135) | copy-start | bytes 7077892
  145.2 7.8 %copy-start.10 = (bf16[3072,512]{1,0:T(8,128)(2,1)S(1)}, bf16[3072,512]{1,0:T(8,128)(2,1)}, u32[]{:S(2)}) copy-start(bf16[3072,512]{1,0:T(8,128)(2,1)} %param.11) | copy-start | bytes 9437188
  145.2 7.8 %copy-start.16 = (bf16[1,768,768]{2,1,0:T(8,128)(2,1)S(1)}, bf16[1,768,768]{2,1,0:T(8,128)(2,1)}, u32[]{:S(2)}) copy-start(bf16[1,768,768]{2,1,0:T(8,128)(2,1)} %get-tuple-element.214) | copy-start | bytes 3538948
  145.2 7.8 %copy-start.17 = (bf16[1,768,768]{2,1,0:T(8,128)(2,1)S(1)}, bf16[1,768,768]{2,1,0:T(8,128)(2,1)}, u32[]{:S(2)}) copy-start(bf16[1,768,768]{2,1,0:T(8,128)(2,1)} %get-tuple-element.215) | copy-start | bytes 3538948
  145.2 7.8 %copy-start.18 = (bf16[1,768,768]{2,1,0:T(8,128)(2,1)S(1)}, bf16[1,768,768]{2,1,0:T(8,128)(2,1)}, u32[]{:S(2)}) copy-start(bf16[1,768,768]{2,1,0:T(8,128)(2,1)} %get-tuple-element.216) | copy-start | bytes 3538948
  145.3 7.8 %copy-start.19 = (bf16[1,768,768]{2,1,0:T(8,128)(2,1)S(1)}, bf16[1,768,768]{2,1,0:T(8,128)(2,1)}, u32[]{:S(2)}) copy-start(bf16[1,768,768]{2,1,0:T(8,128)(2,1)} %get-tuple-element.217) | copy-start | bytes 3538948
  153.1 4.9 %copy-start.28 = (f32[1,1,32]{2,1,0:T(1,128)S(1)}, f32[1,1,32]{2,1,0:T(1,128)}, u32[]{:S(2)}) copy-start(f32[1,1,32]{2,1,0:T(1,128)} %get-tuple-element.199) | copy-start | bytes 388
  153.1 28.0 %copy-start.29 = (s32[512]{0:T(512)S(1)}, s32[512]{0:T(512)}, u32[]{:S(2)}) copy-start(s32[512]{0:T(512)} %param.15) | copy-start | bytes 6148
  153.1 32.3 %copy-start.23 = (f32[32]{0:T(128)S(1)}, f32[32]{0:T(128)}, u32[]{:S(2)}) copy-start(f32[32]{0:T(128)} %copy-done.22) | copy-start | bytes 388
  153.1 32.3 %copy-start.27 = (f32[32]{0:T(128)S(1)}, f32[32]{0:T(128)}, u32[]{:S(2)}) copy-start(f32[32]{0:T(128)} %copy-done.26) | copy-start | bytes 388
  181.1 9.3 %copy-start.5 = (f32[4,768,512]{2,1,0:T(8,128)S(1)}, f32[4,768,512]{2,1,0:T(8,128)}, u32[]{:S(2)}) copy-start(f32[4,768,512]{2,1,0:T(8,128)} %fusion.34) | copy-start | bytes 18874372
  181.1 9.3 %copy-start.9 = (f32[4,768,32]{1,2,0:T(8,128)S(1)}, f32[4,768,32]{1,2,0:T(8,128)}, u32[]{:S(2)}) copy-start(f32[4,768,32]{1,2,0:T(8,128)} %copy-done.8) | copy-start | bytes 1179652
  181.1 12.8 %copy-start.25 = (f32[32]{0:T(128)S(1)}, f32[32]{0:T(128)}, u32[]{:S(2)}) copy-start(f32[32]{0:T(128)} %copy-done.24) | copy-start | bytes 388
  211.3 8.1 %copy-start.7 = (f32[4,768,32]{1,2,0:T(8,128)S(1)}, f32[4,768,32]{1,2,0:T(8,128)}, u32[]{:S(2)}) copy-start(f32[4,768,32]{1,2,0:T(8,128)} %copy-done.6) | copy-start | bytes 1179652
  211.4 15.6 %copy-start.1 = (f32[1,768,512]{2,1,0:T(8,128)S(1)}, f32[1,768,512]{2,1,0:T(8,128)}, u32[]{:S(2)}) copy-start(f32[1,768,512]{2,1,0:T(8,128)} %fusion.23) | copy-start | bytes 4718596
  211.4 15.6 %copy-start.2 = (f32[1,768,512]{2,1,0:T(8,128)S(1)}, f32[1,768,512]{2,1,0:T(8,128)}, u32[]{:S(2)}) copy-start(f32[1,768,512]{2,1,0:T(8,128)} %fusion.17) | copy-start | bytes 4718596
  211.5 15.6 %copy-start.3 = (f32[1,768,512]{2,1,0:T(8,128)S(1)}, f32[1,768,512]{2,1,0:T(8,128)}, u32[]{:S(2)}) copy-start(f32[1,768,512]{2,1,0:T(8,128)} %fusion.20) | copy-start | bytes 4718596
  211.5 15.5 %copy-start.4 = (f32[1,768,512]{2,1,0:T(8,128)S(1)}, f32[1,768,512]{2,1,0:T(8,128)}, u32[]{:S(2)}) copy-start(f32[1,768,512]{2,1,0:T(8,128)} %fusion.14) | copy-start | bytes 4718596
Sparse Core Ops, SparseCore 0:
  31.1 40.6 all-gather.3
  73.9 36.8 all-gather.5
where the time goes:
time: 305 us; the launch traced here: 303 us
  other arithmetic  152 us (50%)
  blocking collectives  82.4 us (27%)
  matrix products  46.8 us (15%)
  between operations  14.4 us (5%)
  local copies, waits for them, and re-layouts  7.32 us (2%)
    reduce_sum x2, other arithmetic, body(): jnp.sum(gain_part[:, None, None] * jnp.exp(-rate_part[:, None, None] * sp...  94.9 us
    pmax x1, blocking collectives, body(): highest = lax.pmax(local_high, 'tm')  29.8 us
    psum x1, blocking collectives, body(): amount = lax.psum(jnp.sum(jnp.exp(scores - highest), axis=(0, 1)), 'tm')  29.5 us
    all_gather x1, blocking collectives, entering(): gathered = jax.tree.map(lambda a: lax.all_gather(a, axis), part)  23.1 us
    convert_element_type x2, other arithmetic, body(): kernel_list.append(block_kernel.astype(jnp.bfloat16))  16.1 us
    dot_general x4, matrix products, body(): jnp.dot(back_table[position], adjoint_state, precision=lax.Precision.HIGH...  15.5 us
    dot_general x4, matrix products, body(): jnp.dot(start_table[position], mode_state, precision=lax.Precision.HIGHES...  15.2 us
    add x15, other arithmetic, combine_states(): return (earlier[0] * latter[0], latter[0][:, None] * earlier[1] + latter[1])  13.8 us
  transfers between devices with their start and end apart: 2, of which 0 were waited for; matrix products, arithmetic and copies ran while one was open for 47% of the time, Pallas kernels for 0%

commit v1 on v0

--- a/solution.py
+++ b/solution.py
@@ -111,7 +111,7 @@
     scores = SHARPNESS * stress_full
     local_high = jnp.max(scores, axis=(0, 1))
     highest = lax.pmax(local_high, "tm")
-    amount = lax.psum(jnp.sum(jnp.exp(scores - highest), axis=(0, 1)), "tm")
+    amount = jnp.sum(lax.all_gather(jnp.sum(jnp.exp(scores - highest), axis=(0, 1)), "tm"), axis=0)
     softened_peak_tension = (highest + jnp.log(amount)) / SHARPNESS
     adjoint_state = adjoint_in
     reversed_blocks = []

time: 305 us -> 293 us (0.961)
  blocking collectives: 82.4 us -> 70.1 us
    psum x1 -> x0, blocking collectives: 29.5 us -> none  [body(): amount = lax.psum(jnp.sum(jnp.exp(scores - highest), axis=(0, 1)), 'tm')]
    all_gather x0 -> x1, blocking collectives: none -> 17.2 us  [body(): lax.all_gather(jnp.sum(jnp.exp(scores - highest), axis=(0, 1)), 'tm')]
  transfers between devices with their start and end apart: 2 -> 2, of which waited for: 0 -> 0; matrix products, arithmetic and copies ran while one was open for 47% -> 49% of each run, Pallas kernels for 0% -> 0%
where the time goes in v1:
time: 293 us; the launch traced here: 291 us
  other arithmetic  152 us (52%)
  blocking collectives  70.1 us (24%)
  matrix products  46.8 us (16%)
  between operations  14.4 us (5%)
  local copies, waits for them, and re-layouts  7.32 us (2%)
    reduce_sum x2, other arithmetic, body(): jnp.sum(gain_part[:, None, None] * jnp.exp(-rate_part[:, None, None] * sp...  94.9 us
    pmax x1, blocking collectives, body(): highest = lax.pmax(local_high, 'tm')  29.8 us
    all_gather x1, blocking collectives, entering(): gathered = jax.tree.map(lambda a: lax.all_gather(a, axis), part)  23.1 us
    all_gather x1, blocking collectives, body(): lax.all_gather(jnp.sum(jnp.exp(scores - highest), axis=(0, 1)), 'tm')  17.2 us
    convert_element_type x2, other arithmetic, body(): kernel_list.append(block_kernel.astype(jnp.bfloat16))  16.1 us
    dot_general x4, matrix products, body(): jnp.dot(back_table[position], adjoint_state, precision=lax.Precision.HIGH...  15.5 us
    dot_general x4, matrix products, body(): jnp.dot(start_table[position], mode_state, precision=lax.Precision.HIGHES...  15.2 us
    add x15, other arithmetic, combine_states(): return (earlier[0] * latter[0], latter[0][:, None] * earlier[1] + latter[1])  13.8 us
  transfers between devices with their start and end apart: 2, of which 0 were waited for; matrix products, arithmetic and copies ran while one was open for 49% of the time, Pallas kernels for 0%

profile of v1, /device:TPU:0, one launch (start us, length us, event | category | flops | bytes accessed | tf_op | source)
XLA Modules:
  0.0 291.0 jit_solution(3093160504681461550)
XLA Ops:
  7.2 2.1 reshape.270
  9.4 2.0 copy.54
  11.4 12.3 %reduce-window.6 = f32[32,4,6,128]{3,0,1,2:T(8,128)S(1)} reduce-window(f32[32,4,6,128]{3,0,1,2:T(8,128)} %copy.54, f32[]{:T(128)} %constant.65.clone.1), window={size=1x1x1x128 pad=0_0x0_0x0_0x127_0}, to_apply=%region_0.0 | reduce-window | flops 12484608 | bytes 786436 | tf_op jit(solution)/shard_map/reduce-window
  24.4 0.7 fusion.53
  26.0 2.8 fusion.41
  29.4 0.7 copy-done.14
  30.1 0.8 slice_add_fusion
  31.0 0.7 all-gather.8.cloned.1.call-update
  31.7 1.6 slice_bitcast_fusion.27
  33.4 0.6 slice_negate_fusion.3
  34.3 22.8 %multiply_reduce_fusion.15 = (f32[768,768]{1,0:T(8,128)}, f32[768,768]{1,0:T(8,128)}, f32[768,768]{1,0:T(8,128)}, f32[768,768]{1,0:T(8,128)}) fusion(f32[8,768]{1,0:T(8,128)S(1)} %get-tuple-element.194, f32[8]{0:T(128)S(1)} %get-tuple-element.210, f32[8]{0:T(128)S(1)} %get-tuple-element.206, pred[768,768]{1,0:T(8,128)(4,1)S(1)} %iota_compare_fusion, ...), kind=kLoop, calls=%fused_computation.19 | loop fusion | flops 92012544 | bytes 10125376 | tf_op jit(solution)/shard_map/reduce_sum | solution.py:54
  57.0 72.1 %multiply_reduce_fusion.14 = (f32[768,768]{1,0:T(8,128)}, f32[768,768]{1,0:T(8,128)}, f32[768,768]{1,0:T(8,128)}, f32[768,768]{1,0:T(8,128)}, f32[768,768]{1,0:T...) fusion(f32[8,768]{1,0:T(8,128)} %get-tuple-element.193, ...), kind=kLoop, calls=%fused_computation.18 | loop fusion | flops 276037632 | bytes 29196480 | tf_op jit(solution)/shard_map/reduce_sum | solution.py:54
  129.1 9.0 %fusion.28 = (bf16[1,768,768]{2,1,0:T(8,128)(2,1)}, bf16[1,768,768]{2,1,0:T(8,128)(2,1)}) fusion(f32[768,768]{1,0:T(8,128)} %get-tuple-element.156, f32[768,768]{1,0:T(8,128)} %get-tuple-element.152, f32[768,768]{1,0:T(8,128)} %get-tuple-element.137, f32[768,768]{1,0:T(8,128)} %get-tuple-element.133, f32[768,768]{1,0:T(8,128)} %get-tuple-element.155, ...), kind=kLoop, calls=%fused_computation.66 | loop fusion | flops 4718592 | bytes 21233664 | tf_op jit(solution)/shard_map/convert_element_type | solution.py:57
  138.1 7.1 %fusion.30 = (bf16[1,768,768]{2,1,0:T(8,128)(2,1)}, bf16[1,768,768]{2,1,0:T(8,128)(2,1)}) fusion(f32[768,768]{1,0:T(8,128)} %get-tuple-element.154, f32[768,768]{1,0:T(8,128)} %get-tuple-element.150, f32[768,768]{1,0:T(8,128)S(1)} %copy-done.11, f32[768,768]{1,0:T(8,128)S(1)} %copy-done.13, f32[768,768]{1,0:T(8,128)} %get-tuple-element.153, ...), kind=kLoop, calls=%fused_computation.68 | loop fusion | flops 4718592 | bytes 21233664 | tf_op jit(solution)/shard_map/convert_element_type | solution.py:57
  145.3 7.8 %fusion.34 = f32[4,768,512]{2,1,0:T(8,128)} fusion(bf16[4,768,512]{2,1,0:T(8,128)(2,1)S(1)} %bitcast.252, bf16[1,768,768]{2,1,0:T(8,128)(2,1)} %get-tuple-element.217, bf16[1,768,768]{2,1,0:T(8,128)(2,1)} %get-tuple-element.216, bf16[1,768,768]{2,1,0:T(8,128)(2,1)} %get-tuple-element.215, bf16[1,768,768]{2,1,0:T(8,128)(2,1)} %get-tuple-element.214), kind=kOutput, calls=%fused_computation.72 | convolution fusion | flops 2422996992 | bytes 14155776 | tf_op jit(solution)/shard_map/bts,bsw->btw/dot_general | solution.py:64
  153.1 4.8 %fusion.33 = f32[4,768,512]{2,1,0:T(8,128)} fusion(bf16[4,768,512]{2,1,0:T(8,128)(2,1)S(1)} %bitcast.256, bf16[1,768,768]{2,1,0:T(8,128)(2,1)S(1)} %copy-done.19, bf16[1,768,768]{2,1,0:T(8,128)(2,1)S(1)} %copy-done.18, bf16[1,768,768]{2,1,0:T(8,128)(2,1)S(1)} %copy-done.17, bf16[1,768,768]{2,1,0:T(8,128)(2,1)S(1)} %copy-done.16), kind=kOutput, calls=%fused_computation.71 | convolution fusion | flops 2422996992 | bytes 14155776 | tf_op jit(solution)/shard_map/bts,btw->bsw/dot_general | solution.py:71
  157.9 23.1 %all-gather.1 = f32[16,1,32]{2,1,0:T(1,128)S(1)} all-gather(f32[1,1,32]{2,1,0:T(1,128)S(1)} %copy-done.28), channel_id=1, replica_groups=mesh['parts'=2,'tm'=16] {'tm'}, dimensions={0}, use_global_device_ids=true | all-gather | bytes 2176 | tf_op jit(solution)/shard_map/all_gather | solution.py:15
  181.1 4.3 %fusion.23 = f32[1,768,512]{2,1,0:T(8,128)} fusion(f32[4,768,512]{2,1,0:T(8,128)} %fusion.34, f32[32,512]{1,0:T(8,128)S(1)} %get-tuple-element.131, f32[512]{0:T(512)S(1)} %convert_multiply_fusion, f32[4,768,32]{1,2,0:T(8,128)} %copy-done.8), kind=kOutput, calls=%fused_computation.61 | convolution fusion | flops 151781376 | bytes 3311616 | tf_op jit(solution)/shard_map/dot_general | solution.py:101
  185.4 1.0 bitcast_add_fusion.8
  186.3 4.1 %fusion.17 = f32[1,768,512]{2,1,0:T(8,128)} fusion(f32[4,768,512]{2,1,0:T(8,128)} %fusion.34, f32[32,512]{1,0:T(8,128)S(1)} %bitcast_add_fusion.8, f32[512]{0:T(512)S(1)} %convert_multiply_fusion, f32[4,768,32]{1,2,0:T(8,128)} %copy-done.8), kind=kOutput, calls=%fused_computation.53 | convolution fusion | flops 151781376 | bytes 3311616 | tf_op jit(solution)/shard_map/dot_general | solution.py:101
  190.4 3.5 %fusion.20 = f32[1,768,512]{2,1,0:T(8,128)} fusion(f32[4,768,512]{2,1,0:T(8,128)S(1)} %copy-done.5, f32[512]{0:T(512)S(1)} %convert_multiply_fusion, f32[4,768,32]{1,2,0:T(8,128)S(1)} %copy-done.9, f32[32,512]{1,0:T(8,128)S(1)} %get-tuple-element.131, f32[4,32,512]{2,1,0:T(8,128)} %copy-done.14, f32[32]{0:T(128)S(1)} %copy-done.27), kind=kOutput, calls=%fused_computation.57 | convolution fusion | flops 151814144 | bytes 3377664 | tf_op jit(solution)/shard_map/dot_general | solution.py:101
  193.9 3.5 %fusion.14 = f32[1,768,512]{2,1,0:T(8,128)} fusion(f32[4,768,512]{2,1,0:T(8,128)S(1)} %copy-done.5, f32[512]{0:T(512)S(1)} %convert_multiply_fusion, f32[4,768,32]{1,2,0:T(8,128)S(1)} %copy-done.9, f32[32,512]{1,0:T(8,128)S(1)} %bitcast_add_fusion.8, f32[4,32,512]{2,1,0:T(8,128)} %copy-done.14, f32[32]{0:T(128)S(1)} %copy-done.25), kind=kOutput, calls=%fused_computation.49 | convolution fusion | flops 151814144 | bytes 3377664 | tf_op jit(solution)/shard_map/dot_general | solution.py:101
  197.3 14.0 %while.27 = (s32[]{:T(128)}, f32[32,512]{1,0:T(8,128)S(1)}, s32[]{:T(128)}, f32[16,32]{1,0:T(8,128)S(1)}, f32[16,32,512]{2,1,0:T(8,128)}, /*index=5*/s32[]{:T(128)}, s32[]{:T(128)}, s32[]{:T(128)}, s32[]{:T(128)}) while((s32[]{:T(128)}, f32[32,512]{1,0:T(8,128)S(1)}, s32[]{:T(128)}, f32[16,32]{1,0:T(8,128)S(1)}, f32[16,32,512]{2,1,0:T(8,128)}, ...), condition=%wide.region_21.22_spmd, body=%wide.region_20.21_spmd.sunk | while | flops 32774 | bytes 197139 | solution.py:24
  197.4 0.9 bitcast_add_fusion.15
  198.3 0.9 bitcast_add_fusion.15
  199.2 0.9 bitcast_add_fusion.15
  200.2 0.9 bitcast_add_fusion.15
  201.1 0.9 bitcast_add_fusion.15
  202.0 0.9 bitcast_add_fusion.15
  203.0 0.9 bitcast_add_fusion.15
  203.9 0.9 bitcast_add_fusion.15
  204.8 0.9 bitcast_add_fusion.15
  205.8 0.9 bitcast_add_fusion.15
  206.7 0.9 bitcast_add_fusion.15
  207.6 0.9 bitcast_add_fusion.15
  208.6 0.9 bitcast_add_fusion.15
  209.5 0.9 bitcast_add_fusion.15
  210.4 0.9 bitcast_add_fusion.15
  211.5 4.1 %fusion.24 = bf16[1,768,512]{2,1,0:T(8,128)(2,1)} fusion(f32[4,768,512]{2,1,0:T(8,128)} %fusion.33, f32[512]{0:T(512)S(1)} %convert_multiply_fusion, f32[4,768,32]{1,2,0:T(8,128)} %copy-done.6, f32[32,512]{1,0:T(8,128)S(1)} %bitcast_add_fusion.4, f32[4,32,512]{2,1,0:T(8,128)S(1)} %fusion.41, f32[32]{0:T(128)S(1)} %copy-done.23), kind=kOutput, calls=%fused_computation.62 | convolution fusion | flops 152207360 | bytes 2591232 | tf_op jit(solution)/shard_map/dot_general | solution.py:119
  215.5 3.9 %fusion.25 = bf16[1,768,512]{2,1,0:T(8,128)(2,1)} fusion(f32[32,512]{1,0:T(8,128)S(1)} %bitcast_add_fusion.4, f32[4,768,512]{2,1,0:T(8,128)} %fusion.33, f32[512]{0:T(512)S(1)} %convert_multiply_fusion, f32[4,768,32]{1,2,0:T(8,128)} %copy-done.6), kind=kOutput, calls=%fused_computation.63 | convolution fusion | flops 152174592 | bytes 2525184 | tf_op jit(solution)/shard_map/dot_general | solution.py:119
  219.4 3.8 %fusion.26 = bf16[1,768,512]{2,1,0:T(8,128)(2,1)} fusion(f32[4,768,512]{2,1,0:T(8,128)} %fusion.33, f32[512]{0:T(512)S(1)} %convert_multiply_fusion, f32[4,768,32]{1,2,0:T(8,128)S(1)} %copy-done.7, f32[32,512]{1,0:T(8,128)S(1)} %get-tuple-element.132, f32[4,32,512]{2,1,0:T(8,128)S(1)} %fusion.41, f32[32]{0:T(128)S(1)} %get-tuple-element.198), kind=kOutput, calls=%fused_computation.64 | convolution fusion | flops 152207360 | bytes 2591232 | tf_op jit(solution)/shard_map/dot_general | solution.py:119
  223.2 3.8 %fusion.27 = bf16[1,768,512]{2,1,0:T(8,128)(2,1)} fusion(f32[32,512]{1,0:T(8,128)S(1)} %get-tuple-element.132, f32[4,768,512]{2,1,0:T(8,128)} %fusion.33, f32[512]{0:T(512)S(1)} %convert_multiply_fusion, f32[4,768,32]{1,2,0:T(8,128)S(1)} %copy-done.7), kind=kOutput, calls=%fused_computation.65 | convolution fusion | flops 152174592 | bytes 2525184 | tf_op jit(solution)/shard_map/dot_general | solution.py:119
  227.0 0.9 multiply_reduce_fusion.16
  227.9 2.1 fusion.32
  229.9 29.8 %pmax.7 = f32[512]{0:T(512)S(1)} all-reduce(f32[512]{0:T(512)S(1)} %multiply_reduce_fusion.16), channel_id=1, replica_groups=mesh['parts'=2,'tm'=16] {'tm'}, use_global_device_ids=true, to_apply=%region_23.24 | all-reduce | flops 512 | bytes 4096 | tf_op jit(solution)/shard_map/pmax | solution.py:113
  259.7 3.4 %exponential_reduce_fusion = f32[512]{0:T(512)S(1)} fusion(f32[512]{0:T(512)S(1)} %pmax.7, f32[1,768,512]{2,1,0:T(8,128)} %fusion.14, f32[1,768,512]{2,1,0:T(8,128)} %fusion.17, f32[1,768,512]{2,1,0:T(8,128)} %fusion.20, f32[1,768,512]{2,1,0:T(8,128)} %fusion.23), kind=kLoop, calls=%fused_computation.21 | loop fusion | flops 9436672 | bytes 6295552 | tf_op jit(solution)/shard_map/reduce_sum | solution.py:114
  263.1 17.2 %all-gather.2 = f32[16,1,512]{2,1,0:T(1,128)S(1)} all-gather(f32[1,1,512]{2,1,0:T(1,128)S(1)} %bitcast.258), channel_id=2, replica_groups=mesh['parts'=2,'tm'=16] {'tm'}, dimensions={0}, use_global_device_ids=true | all-gather | bytes 34816 | tf_op jit(solution)/shard_map/all_gather | solution.py:114
  281.0 3.2 %pad_maximum_fusion.2 = bf16[4,768,512]{2,1,0:T(8,128)(2,1)} fusion(bf16[1,768,512]{2,1,0:T(8,128)(2,1)} %fusion.27, bf16[1,768,512]{2,1,0:T(8,128)(2,1)} %fusion.26, bf16[1,768,512]{2,1,0:T(8,128)(2,1)} %fusion.25, bf16[1,768,512]{2,1,0:T(8,128)(2,1)} %fusion.24), kind=kLoop, calls=%fused_computation.24 | loop fusion | flops 4718592 | bytes 6291456 | tf_op jit(solution)/shard_map/stack | solution.py:130
  (100 shorter events, 3.5 us)
Async XLA Ops:
  7.2 21.6 %copy-start = (bf16[3072,512]{1,0:T(8,128)(2,1)S(1)}, bf16[3072,512]{1,0:T(8,128)(2,1)}, u32[]{:S(2)}) copy-start(bf16[3072,512]{1,0:T(8,128)(2,1)} %param.10) | copy-start | bytes 9437188
  7.2 173.9 %all-gather.6.cloned.1.call-start = ((), (), s32[]{:S(2)}) async-start(), calls=%async_computation | async-start | bytes 1114112 | tf_op jit(solution)/shard_map/all_gather | solution.py:15
  24.2 1.7 copy-start.15
  25.7 5.2 %copy-start.22 = (f32[32]{0:T(128)}, f32[32]{0:T(128)S(1)}, u32[]{:S(2)}) copy-start(f32[32]{0:T(128)S(1)} %get-tuple-element.201) | copy-start | bytes 388
  25.7 5.2 %copy-start.24 = (f32[32]{0:T(128)}, f32[32]{0:T(128)S(1)}, u32[]{:S(2)}) copy-start(f32[32]{0:T(128)S(1)} %get-tuple-element.200) | copy-start | bytes 388
  25.7 5.2 %copy-start.26 = (f32[32]{0:T(128)}, f32[32]{0:T(128)S(1)}, u32[]{:S(2)}) copy-start(f32[32]{0:T(128)S(1)} %get-tuple-element.197) | copy-start | bytes 388
  25.9 2.9 copy-start.6
  25.9 3.5 %copy-start.8 = (f32[4,768,32]{1,2,0:T(8,128)}, f32[4,768,32]{1,2,0:T(8,128)S(1)}, u32[]{:S(2)}) copy-start(f32[4,768,32]{1,2,0:T(8,128)S(1)} %get-tuple-element.178) | copy-start | bytes 1179652
  25.9 7.5 %copy-start.21 = (f32[32]{0:T(128)S(1)}, f32[32]{0:T(128)}, u32[]{:S(2)}) copy-start(f32[32]{0:T(128)} %param.13) | copy-start | bytes 388
  29.4 0.7 copy-start.14
  30.9 166.4 %all-gather.8.cloned.1.call-start = ((), (), s32[]{:S(2)}) async-start(), calls=%async_computation.1 | async-start | bytes 1114112 | tf_op jit(solution)/shard_map/all_gather | solution.py:15
  34.2 22.8 %copy-start.20 = (pred[768,768]{1,0:T(8,128)(4,1)}, pred[768,768]{1,0:T(8,128)(4,1)S(1)}, u32[]{:S(2)}) copy-start(pred[768,768]{1,0:T(8,128)(4,1)S(1)} %iota_compare_fusion) | copy-start | bytes 1769476
  34.2 22.8 %copy-start.30 = (f32[8]{0:T(128)S(1)}, f32[8]{0:T(128)}, u32[]{:S(2)}) copy-start(f32[8]{0:T(128)} %get-tuple-element.212) | copy-start | bytes 100
  129.1 9.0 %copy-start.11 = (f32[768,768]{1,0:T(8,128)S(1)}, f32[768,768]{1,0:T(8,128)}, u32[]{:S(2)}) copy-start(f32[768,768]{1,0:T(8,128)} %get-tuple-element.139) | copy-start | bytes 7077892
  129.1 9.0 %copy-start.12 = (f32[768,768]{1,0:T(8,128)S(1)}, f32[768,768]{1,0:T(8,128)}, u32[]{:S(2)}) copy-start(f32[768,768]{1,0:T(8,128)} %get-tuple-element.140) | copy-start | bytes 7077892
  129.1 9.0 %copy-start.13 = (f32[768,768]{1,0:T(8,128)S(1)}, f32[768,768]{1,0:T(8,128)}, u32[]{:S(2)}) copy-start(f32[768,768]{1,0:T(8,128)} %get-tuple-element.135) | copy-start | bytes 7077892
  145.2 7.8 %copy-start.10 = (bf16[3072,512]{1,0:T(8,128)(2,1)S(1)}, bf16[3072,512]{1,0:T(8,128)(2,1)}, u32[]{:S(2)}) copy-start(bf16[3072,512]{1,0:T(8,128)(2,1)} %param.11) | copy-start | bytes 9437188
  145.2 7.8 %copy-start.16 = (bf16[1,768,768]{2,1,0:T(8,128)(2,1)S(1)}, bf16[1,768,768]{2,1,0:T(8,128)(2,1)}, u32[]{:S(2)}) copy-start(bf16[1,768,768]{2,1,0:T(8,128)(2,1)} %get-tuple-element.214) | copy-start | bytes 3538948
  145.2 7.8 %copy-start.17 = (bf16[1,768,768]{2,1,0:T(8,128)(2,1)S(1)}, bf16[1,768,768]{2,1,0:T(8,128)(2,1)}, u32[]{:S(2)}) copy-start(bf16[1,768,768]{2,1,0:T(8,128)(2,1)} %get-tuple-element.215) | copy-start | bytes 3538948
  145.2 7.8 %copy-start.18 = (bf16[1,768,768]{2,1,0:T(8,128)(2,1)S(1)}, bf16[1,768,768]{2,1,0:T(8,128)(2,1)}, u32[]{:S(2)}) copy-start(bf16[1,768,768]{2,1,0:T(8,128)(2,1)} %get-tuple-element.216) | copy-start | bytes 3538948
  145.3 7.8 %copy-start.19 = (bf16[1,768,768]{2,1,0:T(8,128)(2,1)S(1)}, bf16[1,768,768]{2,1,0:T(8,128)(2,1)}, u32[]{:S(2)}) copy-start(bf16[1,768,768]{2,1,0:T(8,128)(2,1)} %get-tuple-element.217) | copy-start | bytes 3538948
  153.1 4.9 %copy-start.28 = (f32[1,1,32]{2,1,0:T(1,128)S(1)}, f32[1,1,32]{2,1,0:T(1,128)}, u32[]{:S(2)}) copy-start(f32[1,1,32]{2,1,0:T(1,128)} %get-tuple-element.199) | copy-start | bytes 388
  153.1 28.0 %copy-start.29 = (s32[512]{0:T(512)S(1)}, s32[512]{0:T(512)}, u32[]{:S(2)}) copy-start(s32[512]{0:T(512)} %param.15) | copy-start | bytes 6148
  153.1 32.3 %copy-start.23 = (f32[32]{0:T(128)S(1)}, f32[32]{0:T(128)}, u32[]{:S(2)}) copy-start(f32[32]{0:T(128)} %copy-done.22) | copy-start | bytes 388
  153.1 32.3 %copy-start.27 = (f32[32]{0:T(128)S(1)}, f32[32]{0:T(128)}, u32[]{:S(2)}) copy-start(f32[32]{0:T(128)} %copy-done.26) | copy-start | bytes 388
  181.1 9.3 %copy-start.5 = (f32[4,768,512]{2,1,0:T(8,128)S(1)}, f32[4,768,512]{2,1,0:T(8,128)}, u32[]{:S(2)}) copy-start(f32[4,768,512]{2,1,0:T(8,128)} %fusion.34) | copy-start | bytes 18874372
  181.1 9.3 %copy-start.9 = (f32[4,768,32]{1,2,0:T(8,128)S(1)}, f32[4,768,32]{1,2,0:T(8,128)}, u32[]{:S(2)}) copy-start(f32[4,768,32]{1,2,0:T(8,128)} %copy-done.8) | copy-start | bytes 1179652
  181.1 12.8 %copy-start.25 = (f32[32]{0:T(128)S(1)}, f32[32]{0:T(128)}, u32[]{:S(2)}) copy-start(f32[32]{0:T(128)} %copy-done.24) | copy-start | bytes 388
  211.3 8.1 %copy-start.7 = (f32[4,768,32]{1,2,0:T(8,128)S(1)}, f32[4,768,32]{1,2,0:T(8,128)}, u32[]{:S(2)}) copy-start(f32[4,768,32]{1,2,0:T(8,128)} %copy-done.6) | copy-start | bytes 1179652
  211.4 15.6 %copy-start.1 = (f32[1,768,512]{2,1,0:T(8,128)S(1)}, f32[1,768,512]{2,1,0:T(8,128)}, u32[]{:S(2)}) copy-start(f32[1,768,512]{2,1,0:T(8,128)} %fusion.23) | copy-start | bytes 4718596
  211.4 15.6 %copy-start.2 = (f32[1,768,512]{2,1,0:T(8,128)S(1)}, f32[1,768,512]{2,1,0:T(8,128)}, u32[]{:S(2)}) copy-start(f32[1,768,512]{2,1,0:T(8,128)} %fusion.17) | copy-start | bytes 4718596
  211.5 15.6 %copy-start.3 = (f32[1,768,512]{2,1,0:T(8,128)S(1)}, f32[1,768,512]{2,1,0:T(8,128)}, u32[]{:S(2)}) copy-start(f32[1,768,512]{2,1,0:T(8,128)} %fusion.20) | copy-start | bytes 4718596
  211.5 15.5 %copy-start.4 = (f32[1,768,512]{2,1,0:T(8,128)S(1)}, f32[1,768,512]{2,1,0:T(8,128)}, u32[]{:S(2)}) copy-start(f32[1,768,512]{2,1,0:T(8,128)} %fusion.14) | copy-start | bytes 4718596
Sparse Core Ops, SparseCore 0:
  31.1 40.6 all-gather.5
  73.9 36.8 all-gather.7
